TPU v7x, 32 devices: a whole 2x2x4 slice. The times are simulated.
32 devices in a mesh: ka: 8 (over z, x), band: 4 (over y, core).
Axes of the slice: x: 2, y: 2, z: 4, core: 2. Of those that a mesh axis runs over, the one named last changes fastest.
Arguments:
- occupied: bfloat16 [16, 8, 4096], P('ka'), may hold values from -6 to 6
- virtual: bfloat16 [16, 128, 4096], P('ka', 'band'), may hold values from -6 to 6
- occ_energy: float32 [16, 8], P('ka'), may hold values from -2 to -0.5
- virt_energy: float32 [16, 128], P(None, 'band'), may hold values from 0.5 to 2
- partner: int32 [2, 16], replicated, may hold values from 0 to 15, as said below
- coulomb: float32 [2, 512], replicated, may hold values from 0.5 to 2
- basis: bfloat16 [512, 4096], replicated, may hold values from -0.09375 to 0.09375
Outputs:
- occ_update: bfloat16 [16, 8, 4096], P('ka', None, 'band')
- virt_update: bfloat16 [16, 128, 4096], P('ka', 'band')
Inputs may be any that keep to these rules, and one draw needn't show every extreme that they name: Each row pairs the 16 k-points: partner[q, partner[q, k]] == k and partner[q, k] != k.
All inputs are finite; a program needn't handle non-finite values.
Results may differ from a plain program's by a relative error of at most 0.012.
Values may be sent and summed in bfloat16 or wider, within the bound.
No kernel may reach another device: no remote copies, remote signals or barrier semaphores. Data moves between devices by JAX's collectives and lax.ppermute only.
A program may use at most 64 MiB of HBM per device.

v0:
```python
import math
import jax
import jax.numpy as jnp
from jax import lax
from jax.sharding import PartitionSpec as P

FREQUENCY = 2.5
BROADENING = 0.4


def response(energy_gaps):
    shifted = FREQUENCY - energy_gaps
    return shifted / (shifted * shifted + BROADENING * BROADENING)


def contract_grid(left, right):
    return lax.dot_general(
        left, right, (((1,), (1,)), ((), ())), preferred_element_type=jnp.float32
    )


def contract_rows(left, right):
    return lax.dot_general(
        left, right, (((0,), (0,)), ((), ())), preferred_element_type=jnp.float32
    )


def shards(occupied, virtual, occ_energy, virt_energy, partner, coulomb, basis):
    local_k, occ_count, grid_count = occupied.shape
    group_count = virtual.shape[1]
    aux_count = basis.shape[0]
    transfers = partner.shape[0]
    ka_size = lax.axis_size("ka")
    band_size = lax.axis_size("band")
    total_k = local_k * ka_size
    virt_count = group_count * band_size
    slice_width = group_count * grid_count // ka_size
    gram_scale = 1.0 / math.sqrt(total_k * occ_count * virt_count * aux_count)
    occ_scale = 1.0 / math.sqrt(transfers * virt_count)
    own_k = lax.axis_index("ka") * local_k + jnp.arange(local_k, dtype=jnp.int32)

    def regroup(slices):
        picked = jnp.stack(
            [jnp.take(slices, partner[transfer], axis=0) for transfer in range(transfers)]
        )
        return lax.all_to_all(picked, "ka", split_axis=1, concat_axis=2, tiled=True)

    routed = regroup(
        lax.all_to_all(
            virtual.reshape(local_k, ka_size, slice_width),
            "ka",
            split_axis=1,
            concat_axis=0,
            tiled=True,
        )
    )
    partner_virt = routed.reshape(transfers, local_k, group_count, grid_count)
    partner_energy = jnp.take(virt_energy, jnp.take(partner, own_k, axis=1), axis=0)
    occ_total = jnp.zeros((local_k, occ_count, grid_count), jnp.float32)
    virt_terms = []
    for transfer in range(transfers):
        pair_rows = (occupied[:, :, None, :] * partner_virt[transfer][:, None, :, :]).reshape(
            -1, grid_count
        )
        project_coeffs = contract_grid(pair_rows, basis).astype(jnp.bfloat16)
        energy_gaps = partner_energy[transfer][:, None, :] - occ_energy[:, :, None]
        weights = response(energy_gaps).reshape(-1, 1)
        weighted = (project_coeffs.astype(jnp.float32) * weights).astype(jnp.bfloat16)
        gram_block = contract_rows(weighted, project_coeffs)
        coul_rows = coulomb[transfer : transfer + 1]
        totals = lax.psum(gram_block[None], ("ka", "band"))
        screen_block = (coul_rows[:, :, None] * totals * coul_rows[:, None, :] * gram_scale).astype(
            jnp.bfloat16
        )[0]
        screened = jnp.dot(project_coeffs, screen_block, preferred_element_type=jnp.float32).astype(
            jnp.bfloat16
        )
        grid_field = jnp.dot(screened, basis, preferred_element_type=jnp.float32).astype(
            jnp.bfloat16
        )
        grid_field = grid_field.reshape(local_k, occ_count, group_count, grid_count).astype(
            jnp.float32
        )
        occ_term = jnp.sum(
            grid_field * partner_virt[transfer][:, None, :, :].astype(jnp.float32), axis=2
        )
        virt_term = jnp.sum(
            grid_field * occupied[:, :, None, :].astype(jnp.float32), axis=1
        ).astype(jnp.bfloat16)
        occ_term, virt_term = (occ_term, virt_term)
        occ_total = occ_total + occ_term
        virt_terms.append(virt_term)
    stacked = jnp.stack(virt_terms).reshape(transfers, local_k, ka_size, slice_width)
    slices = lax.all_to_all(stacked, "ka", split_axis=2, concat_axis=1, tiled=True)
    returned = jnp.take(slices[0], partner[0], axis=0).astype(jnp.float32)
    transfer = 1
    returned = returned + jnp.take(slices[transfer], partner[transfer], axis=0).astype(jnp.float32)
    home_rows = lax.all_to_all(
        returned.astype(jnp.bfloat16), "ka", split_axis=0, concat_axis=1, tiled=True
    )
    virt_update = home_rows.reshape(local_k, group_count, grid_count)
    occ_share = lax.psum_scatter(
        occ_total.astype(jnp.bfloat16), "band", scatter_dimension=2, tiled=True
    ).astype(jnp.float32)
    return ((occ_share * occ_scale).astype(jnp.bfloat16), virt_update)


def solution(mesh):
    in_specs = (
        P("ka", None, None),
        P("ka", "band", None),
        P("ka", None),
        P(None, "band"),
        P(),
        P(),
        P(),
    )
    out_specs = (P("ka", None, "band"), P("ka", "band", None))
    return jax.shard_map(shards, mesh=mesh, in_specs=in_specs, out_specs=out_specs, check_vma=False)
```

profile of v0, /device:TPU:0, one launch (start us, length us, event | category | flops | bytes accessed | tf_op | source)
XLA Modules:
  0.0 310.9 jit_solution(7381379015960021521)
XLA Ops:
  7.2 1.5 reshape.231
  8.6 1.3 copy.50
  10.0 7.3 %all-to-all-start = ((bf16[2,8,16384]{2,0,1:T(2,128)(2,1)}), bf16[2,8,16384]{2,0,1:T(2,128)(2,1)S(1)}, u32[]{:S(2)}, u32[]{:S(2)}) async-start(bf16[2,8,16384]{2,0,1:T(2,128)(2,1)} %copy.50), calls=%async_computation | async-start | bytes 1048576 | tf_op jit(solution)/shard_map/all_to_all | solution.py:49
  17.3 0.8 compare_and_fusion.1
  18.1 13.7 %all-to-all-done = bf16[2,8,16384]{2,0,1:T(2,128)(2,1)S(1)} async-done(((bf16[2,8,16384]{2,0,1:T(2,128)(2,1)}), bf16[2,8,16384]{2,0,1:T(2,128)(2,1)S(1)}, u32[]{:S(2)}, u32[]{:S(2)}) %all-to-all-start) | async-done | bytes 524320 | tf_op jit(solution)/shard_map/all_to_all | solution.py:49
  31.7 0.2 reshape.296
  31.9 0.9 gather_fusion.2
  32.8 0.9 gather_fusion.3
  33.7 0.2 fusion.10
  33.9 0.1 pad_maximum_fusion
  34.0 2.0 copy.51
  36.1 3.6 %all-to-all-start.1 = ((bf16[2,16,1,16384]{3,0,2,1:T(2,128)(2,1)}), bf16[2,16,1,16384]{3,0,2,1:T(2,128)(2,1)S(1)}, u32[]{:S(2)}, u32[]{:S(2)}) async-start(bf16[2,16,1,16384]{3,0,2,1:T(2,128)(2,1)} %copy.51), calls=%async_computation.1 | async-start | bytes 2097152 | tf_op jit(solution)/shard_map/all_to_all | solution.py:46
  39.8 0.1 copy.53
  39.9 0.6 gather_fusion
  40.4 0.1 copy.55
  40.5 0.1 reshape.285
  40.6 0.1 compare_and_fusion.2
  40.7 0.1 copy.54
  40.8 0.6 gather_fusion.1
  41.4 0.1 broadcast_select_fusion
  41.5 0.1 subtract_subtract_fusion
  41.5 0.1 sub.68
  41.6 0.1 sub.63
  41.7 24.0 %all-to-all-done.1 = bf16[2,16,1,16384]{3,0,2,1:T(2,128)(2,1)S(1)} async-done(((bf16[2,16,1,16384]{3,0,2,1:T(2,128)(2,1)}), bf16[2,16,1,16384]{3,0,2,1:T(2,128)(2,1)S(1)}, u32[]{:S(2)}, u32[]{:S(2)}) %all-to-all-start.1) | async-done | bytes 1048608 | tf_op jit(solution)/shard_map/all_to_all | solution.py:46
  65.7 1.7 fusion.32
  67.4 0.6 copy.52
  67.9 0.4 mul.148
  68.4 0.6 copy.56
  68.9 0.4 mul.164
  69.4 0.7 broadcast_multiply_fusion
  70.1 1.4 copy-done.1
  71.6 2.4 convolution_convert_fusion.3
  73.9 2.4 convolution_convert_fusion.5
  76.3 1.6 convolution_bitcast_fusion
  77.9 1.6 convolution_bitcast_fusion.1
  79.5 1.1 convert_element_type.132
  80.6 0.1 convert_element_type.123
  80.7 132.6 %all-reduce.3.cloned.1.call-done = (f32[1,512,512]{2,1,0:T(8,128)}, f32[1,512,512]{2,1,0:T(8,128)}) async-done(((f32[1,512,512]{2,1,0:T(8,128)}, f32[1,512,512]{2,1,0:T(8,128)}), (f32[1,512,512]{2,1,0:T(8,128)}, f32[1,512,512]{2,1,0:T(8,128)})) %all-reduce.3.cloned.1.call-update) | async-done | bytes 2097168 | tf_op jit(solution)/shard_map/psum | solution.py:71
  213.3 7.6 %fusion.2 = (f32[2,8,4096]{2,1,0:T(8,128)S(1)}, bf16[512,4096]{1,0:T(8,128)(2,1)}) fusion(f32[2,32,4096]{2,1,0:T(8,128)} %convert_element_type.132, bf16[512,4096]{1,0:T(8,128)(2,1)} %param.15, bf16[512,512]{1,0:T(8,128)(2,1)S(1)} %convolution_convert_fusion.3, f32[1,512,512]{2,1,0:T(8,128)} %get-tuple-element.6, f32[512]{0:T(512)S(1)} %bitcast.114), kind=kOutput, calls=%fused_computation.12 | convolution fusion | flops 2425552896 | bytes 11274240 | tf_op jit(solution)/shard_map/dot_general | solution.py:78
  220.9 7.6 %fusion = (f32[2,8,4096]{2,1,0:T(8,128)S(1)}, bf16[512,4096]{1,0:T(8,128)(2,1)}) fusion(f32[2,32,4096]{2,1,0:T(8,128)S(1)} %convert_element_type.123, bf16[512,4096]{1,0:T(8,128)(2,1)} %param.15, bf16[512,512]{1,0:T(8,128)(2,1)S(1)} %convolution_convert_fusion.5, f32[1,512,512]{2,1,0:T(8,128)} %get-tuple-element.5, f32[512]{0:T(512)S(1)} %bitcast.113), kind=kOutput, calls=%fused_computation.10 | convolution fusion | flops 2425552896 | bytes 11274240 | tf_op jit(solution)/shard_map/dot_general | solution.py:78
  228.5 4.6 %fusion.1 = (bf16[2,32,4096]{2,1,0:T(8,128)(2,1)S(1)}, bf16[2,32,4096]{2,1,0:T(8,128)(2,1)S(1)}) fusion(bf16[2,8,32,4096]{3,2,1,0:T(8,128)(2,1)} %bitcast.106, f32[2,8,4096]{2,1,0:T(8,128)S(1)} %convert_element_type.136, bf16[2,8,32,4096]{3,2,1,0:T(8,128)(2,1)} %bitcast.105), kind=kLoop, calls=%fused_computation.11 | loop fusion | flops 12058624 | bytes 9699328 | tf_op jit(solution)/shard_map/reduce_sum | solution.py:87
  233.1 0.4 convert_element_type.138
  233.5 0.4 convert_element_type.140
  234.0 0.1 pad_maximum_fusion.1
  234.1 1.1 copy.57
  235.2 28.1 %all_to_all.63 = bf16[2,2,8,16384]{3,1,0,2:T(2,128)(2,1)S(1)} all-to-all(bf16[2,2,8,16384]{3,1,0,2:T(2,128)(2,1)S(1)} %copy.57), channel_id=1, replica_groups=mesh['ka'=8,'band'=4] {'ka'}, dimensions={2} | all-to-all | bytes 2097152 | tf_op jit(solution)/shard_map/all_to_all | solution.py:94
  263.3 0.8 fusion.31
  264.0 0.2 reshape.304
  264.2 0.9 gather_fusion.4
  265.1 0.2 reshape.308
  265.3 0.9 gather_fusion.5
  266.2 0.3 add_convert_fusion
  266.5 0.5 broadcast.260
  267.0 1.0 reduce.1
  268.0 1.1 reshape.317
  269.1 3.6 %all-to-all-start.3 = ((bf16[8,2,16384]{2,1,0:T(2,128)(2,1)}), bf16[8,2,16384]{2,1,0:T(2,128)(2,1)S(1)}, u32[]{:S(2)}, u32[]{:S(2)}) async-start(bf16[8,2,16384]{2,1,0:T(2,128)(2,1)} %reshape.317), calls=%async_computation.4 | async-start | bytes 1048576 | tf_op jit(solution)/shard_map/all_to_all | solution.py:98
  272.8 0.7 add_convert_fusion.1
  273.5 23.5 %reduce-scatter.2.cloned.1.call-done = bf16[2,8,1024]{2,1,0:T(8,128)(2,1)} async-done(((bf16[2,8,4096]{2,1,0:T(8,128)(2,1)}), bf16[2,8,1024]{2,1,0:T(8,128)(2,1)}) %reduce-scatter.2.cloned.1.call-update) | async-done | bytes 32784 | tf_op jit(solution)/shard_map/reduce_scatter | solution.py:102
  297.0 1.4 multiply_convert_fusion.6
  298.4 0.5 reshape.318
  298.9 3.3 %reduce = bf16[16,16384]{1,0:T(8,128)(2,1)S(1)} reduce(bf16[16,1,16384]{2,1,0:T(2,128)(2,1)S(1)} %reshape.318, bf16[]{:T(256)} %constant.60), dimensions={1}, to_apply=%all_to_all.56.reduce_sub_computation | reduce | bytes 1048578 | tf_op jit(solution)/shard_map/all_to_all | solution.py:98
  302.2 0.3 all_to_all.57
  302.5 0.3 copy.59
  302.8 1.2 reshape.232
  (28 shorter events, 0.2 us)
Async XLA Ops:
  7.2 33.6 %copy-start = (f32[16,32]{1,0:T(8,128)S(1)}, f32[16,32]{1,0:T(8,128)}, u32[]{:S(2)}) copy-start(f32[16,32]{1,0:T(8,128)} %param.12) | copy-start | bytes 6148
  10.0 21.8 %all-to-all-start = ((bf16[2,8,16384]{2,0,1:T(2,128)(2,1)}), bf16[2,8,16384]{2,0,1:T(2,128)(2,1)S(1)}, u32[]{:S(2)}, u32[]{:S(2)}) async-start(bf16[2,8,16384]{2,0,1:T(2,128)(2,1)} %copy.50), calls=%async_computation | async-start | bytes 1048576 | tf_op jit(solution)/shard_map/all_to_all | solution.py:49
  33.7 6.0 %copy-start.3 = (s32[2,16]{1,0:T(2,128)S(1)}, s32[2,16]{1,0:T(2,128)}, u32[]{:S(2)}) copy-start(s32[2,16]{1,0:T(2,128)} %param.13) | copy-start | bytes 388
  33.7 7.7 %copy-start.5 = (f32[2,8]{1,0:T(2,128)S(1)}, f32[2,8]{1,0:T(2,128)}, u32[]{:S(2)}) copy-start(f32[2,8]{1,0:T(2,128)} %param.11) | copy-start | bytes 196
  36.1 29.6 %all-to-all-start.1 = ((bf16[2,16,1,16384]{3,0,2,1:T(2,128)(2,1)}), bf16[2,16,1,16384]{3,0,2,1:T(2,128)(2,1)S(1)}, u32[]{:S(2)}, u32[]{:S(2)}) async-start(bf16[2,16,1,16384]{3,0,2,1:T(2,128)(2,1)} %copy.51), calls=%async_computation.1 | async-start | bytes 2097152 | tf_op jit(solution)/shard_map/all_to_all | solution.py:46
  39.7 173.6 %all-reduce.3.cloned.1.call-start = ((), (), s32[]{:S(2)}) async-start(), calls=%async_computation.6 | async-start | bytes 4194304 | tf_op jit(solution)/shard_map/psum | solution.py:71
  65.7 3.7 %copy-start.2 = (bf16[2,8,4096]{2,1,0:T(8,128)(2,1)S(1)}, bf16[2,8,4096]{2,1,0:T(8,128)(2,1)}, u32[]{:S(2)}) copy-start(bf16[2,8,4096]{2,1,0:T(8,128)(2,1)} %param.9) | copy-start | bytes 393220
  69.4 2.2 copy-start.1
  76.3 3.2 %copy-start.4 = (f32[2,512]{1,0:T(2,128)S(1)}, f32[2,512]{1,0:T(2,128)}, u32[]{:S(2)}) copy-start(f32[2,512]{1,0:T(2,128)} %param.14) | copy-start | bytes 12292
  269.1 29.2 %all-to-all-start.3 = ((bf16[8,2,16384]{2,1,0:T(2,128)(2,1)}), bf16[8,2,16384]{2,1,0:T(2,128)(2,1)S(1)}, u32[]{:S(2)}, u32[]{:S(2)}) async-start(bf16[8,2,16384]{2,1,0:T(2,128)(2,1)} %reshape.317), calls=%async_computation.4 | async-start | bytes 1048576 | tf_op jit(solution)/shard_map/all_to_all | solution.py:98
  272.7 24.2 %reduce-scatter.2.cloned.1.call-start = ((), (), s32[]{:S(2)}) async-start(), calls=%async_computation.5 | async-start | bytes 163840 | tf_op jit(solution)/shard_map/reduce_scatter | solution.py:102
Sparse Core Ops, SparseCore 0:
  79.6 133.6 all-reduce.2
  276.0 20.9 reduce-scatter.1
where the time goes:
time: 311 us
  waiting for transfers between devices  194 us (62%)
  blocking collectives  28.1 us (9%)
  matrix products  23 us (7%)
  local copies, waits for them, and re-layouts  22.5 us (7%)
  starting transfers between devices  14.6 us (5%)
  other arithmetic  14.6 us (5%)
  between operations  14.3 us (5%)
    psum x1, waiting for transfers between devices, shards(): totals = lax.psum(gram_block[None], ('ka', 'band'))  133 us
    all_to_all x1, blocking collectives, shards(): lax.all_to_all(stacked, 'ka', split_axis=2, concat_axis=1, tiled=True)  28.1 us
    all_to_all x1, waiting for transfers between devices, regroup(): return lax.all_to_all(picked, 'ka', split_axis=1, concat_axis=2, tiled=True)  24 us
    reduce_scatter x1, waiting for transfers between devices, shards(): lax.psum_scatter(occ_total.astype(jnp.bfloat16), 'band', scatter_dimensio...  23.5 us
    dot_general x2, matrix products, shards(): jnp.dot(screened, basis, preferred_element_type=jnp.float32)  15.2 us
    all_to_all x1, waiting for transfers between devices, shards(): lax.all_to_all(virtual.reshape(local_k, ka_size, slice_width), 'ka', spli...  13.7 us
    all_to_all x1, starting transfers between devices, shards(): lax.all_to_all(virtual.reshape(local_k, ka_size, slice_width), 'ka', spli...  7.28 us
  transfers between devices with their start and end apart: 5, of which 4 were waited for; matrix products, arithmetic and copies ran while one was open for 2% of the time, Pallas kernels for 0%

commit v1 on v0

--- a/solution.py
+++ b/solution.py
@@ -68,7 +68,8 @@
         weighted = (project_coeffs.astype(jnp.float32) * weights).astype(jnp.bfloat16)
         gram_block = contract_rows(weighted, project_coeffs)
         coul_rows = coulomb[transfer : transfer + 1]
-        totals = lax.psum(gram_block[None], ("ka", "band"))
+        values = gram_block[None]
+        totals = jax.lax.psum(jax.lax.psum(values, "band"), "ka")
         screen_block = (coul_rows[:, :, None] * totals * coul_rows[:, None, :] * gram_scale).astype(
             jnp.bfloat16
         )[0]

time: 311 us -> 335 us (1.077)
  waiting for transfers between devices: 194 us -> 216 us
    psum x1 -> x2, waiting for transfers between devices: 133 us -> 155 us  [shards(): totals = jax.lax.psum(jax.lax.psum(values, 'band'), 'ka')]
  transfers between devices with their start and end apart: 5 -> 6, of which waited for: 4 -> 5; matrix products, arithmetic and copies ran while one was open for 2% -> 2% of each run, Pallas kernels for 0% -> 0%
where the time goes in v1:
time: 335 us; the launch traced here: 334 us
  waiting for transfers between devices  216 us (64%)
  blocking collectives  29.4 us (9%)
  matrix products  22.8 us (7%)
  local copies, waits for them, and re-layouts  22.3 us (7%)
  starting transfers between devices  15.3 us (5%)
  other arithmetic  14.6 us (4%)
  between operations  14.1 us (4%)
    psum x2, waiting for transfers between devices, shards(): totals = jax.lax.psum(jax.lax.psum(values, 'band'), 'ka')  155 us
    all_to_all x1, blocking collectives, shards(): lax.all_to_all(stacked, 'ka', split_axis=2, concat_axis=1, tiled=True)  29.4 us
    all_to_all x1, waiting for transfers between devices, regroup(): return lax.all_to_all(picked, 'ka', split_axis=1, concat_axis=2, tiled=True)  23.8 us
    reduce_scatter x1, waiting for transfers between devices, shards(): lax.psum_scatter(occ_total.astype(jnp.bfloat16), 'band', scatter_dimensio...  23.3 us
    dot_general x2, matrix products, shards(): jnp.dot(screened, basis, preferred_element_type=jnp.float32)  15 us
    all_to_all x1, waiting for transfers between devices, shards(): lax.all_to_all(virtual.reshape(local_k, ka_size, slice_width), 'ka', spli...  13.7 us
    all_to_all x1, starting transfers between devices, shards(): lax.all_to_all(virtual.reshape(local_k, ka_size, slice_width), 'ka', spli...  7.28 us
  transfers between devices with their start and end apart: 6, of which 5 were waited for; matrix products, arithmetic and copies ran while one was open for 2% of the time, Pallas kernels for 0%

profile of v1, /device:TPU:0, one launch (start us, length us, event | category | flops | bytes accessed | tf_op | source)
XLA Modules:
  0.0 334.5 jit_solution(12075152669586633961)
XLA Ops:
  7.2 1.5 reshape.231
  8.6 1.3 copy.50
  10.0 7.3 %all-to-all-start = ((bf16[2,8,16384]{2,0,1:T(2,128)(2,1)}), bf16[2,8,16384]{2,0,1:T(2,128)(2,1)S(1)}, u32[]{:S(2)}, u32[]{:S(2)}) async-start(bf16[2,8,16384]{2,0,1:T(2,128)(2,1)} %copy.50), calls=%async_computation | async-start | bytes 1048576 | tf_op jit(solution)/shard_map/all_to_all | solution.py:49
  17.3 0.8 compare_and_fusion.1
  18.1 13.7 %all-to-all-done = bf16[2,8,16384]{2,0,1:T(2,128)(2,1)S(1)} async-done(((bf16[2,8,16384]{2,0,1:T(2,128)(2,1)}), bf16[2,8,16384]{2,0,1:T(2,128)(2,1)S(1)}, u32[]{:S(2)}, u32[]{:S(2)}) %all-to-all-start) | async-done | bytes 524320 | tf_op jit(solution)/shard_map/all_to_all | solution.py:49
  31.7 0.2 reshape.296
  31.9 0.9 gather_fusion.2
  32.8 0.9 gather_fusion.3
  33.7 0.2 fusion.10
  33.9 0.1 pad_maximum_fusion
  34.0 2.0 copy.51
  36.1 3.6 %all-to-all-start.1 = ((bf16[2,16,1,16384]{3,0,2,1:T(2,128)(2,1)}), bf16[2,16,1,16384]{3,0,2,1:T(2,128)(2,1)S(1)}, u32[]{:S(2)}, u32[]{:S(2)}) async-start(bf16[2,16,1,16384]{3,0,2,1:T(2,128)(2,1)} %copy.51), calls=%async_computation.1 | async-start | bytes 2097152 | tf_op jit(solution)/shard_map/all_to_all | solution.py:46
  39.7 0.2 all-reduce.7.cloned.1.call-start
  39.9 0.1 copy.53
  40.0 0.6 gather_fusion
  40.6 0.1 copy.55
  40.7 0.1 reshape.285
  40.9 0.1 copy.54
  41.0 0.6 gather_fusion.1
  41.7 0.1 sub.68
  41.8 0.1 sub.63
  41.9 23.8 %all-to-all-done.1 = bf16[2,16,1,16384]{3,0,2,1:T(2,128)(2,1)S(1)} async-done(((bf16[2,16,1,16384]{3,0,2,1:T(2,128)(2,1)}), bf16[2,16,1,16384]{3,0,2,1:T(2,128)(2,1)S(1)}, u32[]{:S(2)}, u32[]{:S(2)}) %all-to-all-start.1) | async-done | bytes 1048608 | tf_op jit(solution)/shard_map/all_to_all | solution.py:46
  65.6 1.5 fusion.32
  67.2 0.6 copy.52
  67.8 0.4 mul.148
  68.2 0.6 copy.56
  68.8 0.4 mul.164
  69.2 0.7 broadcast_multiply_fusion
  70.0 1.4 copy-done.1
  71.4 2.4 convolution_convert_fusion.3
  73.8 2.4 convolution_convert_fusion.5
  76.1 1.6 convolution_bitcast_fusion
  77.7 1.5 convolution_bitcast_fusion.1
  79.3 0.3 all-reduce.5.cloned.1.call-start
  79.5 50.4 %all-reduce.7.cloned.1.call-done = (f32[1,512,512]{2,1,0:T(8,128)}, f32[1,512,512]{2,1,0:T(8,128)}) async-done(((f32[1,512,512]{2,1,0:T(8,128)}, f32[1,512,512]{2,1,0:T(8,128)}), (f32[1,512,512]{2,1,0:T(8,128)}, f32[1,512,512]{2,1,0:T(8,128)})) %all-reduce.7.cloned.1.call-update) | async-done | bytes 2097168 | tf_op jit(solution)/shard_map/psum | solution.py:72
  130.0 1.1 convert_element_type.132
  131.1 104.9 %all-reduce.5.cloned.1.call-done = (f32[1,512,512]{2,1,0:T(8,128)}, f32[1,512,512]{2,1,0:T(8,128)}) async-done(((f32[1,512,512]{2,1,0:T(8,128)}, f32[1,512,512]{2,1,0:T(8,128)}), (f32[1,512,512]{2,1,0:T(8,128)}, f32[1,512,512]{2,1,0:T(8,128)})) %all-reduce.5.cloned.1.call-update) | async-done | bytes 2097168 | tf_op jit(solution)/shard_map/psum | solution.py:72
  236.0 7.6 %fusion.2 = (f32[2,8,4096]{2,1,0:T(8,128)S(1)}, bf16[512,4096]{1,0:T(8,128)(2,1)}) fusion(f32[2,32,4096]{2,1,0:T(8,128)} %convert_element_type.132, bf16[512,4096]{1,0:T(8,128)(2,1)} %param.15, bf16[512,512]{1,0:T(8,128)(2,1)S(1)} %convolution_convert_fusion.3, f32[1,512,512]{2,1,0:T(8,128)} %get-tuple-element.6, f32[512]{0:T(512)S(1)} %bitcast.114), kind=kOutput, calls=%fused_computation.12 | convolution fusion | flops 2425552896 | bytes 11274240 | tf_op jit(solution)/shard_map/dot_general | solution.py:79
  243.6 7.4 %fusion = (f32[2,8,4096]{2,1,0:T(8,128)S(1)}, bf16[512,4096]{1,0:T(8,128)(2,1)}) fusion(f32[2,32,4096]{2,1,0:T(8,128)S(1)} %convert_element_type.123, bf16[512,4096]{1,0:T(8,128)(2,1)} %param.15, bf16[512,512]{1,0:T(8,128)(2,1)S(1)} %convolution_convert_fusion.5, f32[1,512,512]{2,1,0:T(8,128)} %get-tuple-element.5, f32[512]{0:T(512)S(1)} %bitcast.113), kind=kOutput, calls=%fused_computation.10 | convolution fusion | flops 2425552896 | bytes 11274240 | tf_op jit(solution)/shard_map/dot_general | solution.py:79
  250.9 4.6 %fusion.1 = (bf16[2,32,4096]{2,1,0:T(8,128)(2,1)S(1)}, bf16[2,32,4096]{2,1,0:T(8,128)(2,1)S(1)}) fusion(bf16[2,8,32,4096]{3,2,1,0:T(8,128)(2,1)} %bitcast.106, f32[2,8,4096]{2,1,0:T(8,128)S(1)} %convert_element_type.136, bf16[2,8,32,4096]{3,2,1,0:T(8,128)(2,1)} %bitcast.105), kind=kLoop, calls=%fused_computation.11 | loop fusion | flops 12058624 | bytes 9699328 | tf_op jit(solution)/shard_map/reduce_sum | solution.py:88
  255.6 0.4 convert_element_type.138
  256.0 0.4 convert_element_type.140
  256.4 0.1 pad_maximum_fusion.1
  256.5 1.1 copy.57
  257.6 29.4 %all_to_all.63 = bf16[2,2,8,16384]{3,1,0,2:T(2,128)(2,1)S(1)} all-to-all(bf16[2,2,8,16384]{3,1,0,2:T(2,128)(2,1)S(1)} %copy.57), channel_id=1, replica_groups=mesh['ka'=8,'band'=4] {'ka'}, dimensions={2} | all-to-all | bytes 2097152 | tf_op jit(solution)/shard_map/all_to_all | solution.py:95
  287.1 0.8 fusion.31
  287.8 0.2 reshape.304
  288.0 0.9 gather_fusion.4
  288.9 0.2 reshape.308
  289.1 0.9 gather_fusion.5
  290.0 0.3 add_convert_fusion
  290.3 0.5 broadcast.260
  290.8 1.0 reduce.1
  291.8 1.1 reshape.317
  293.0 3.6 %all-to-all-start.3 = ((bf16[8,2,16384]{2,1,0:T(2,128)(2,1)}), bf16[8,2,16384]{2,1,0:T(2,128)(2,1)S(1)}, u32[]{:S(2)}, u32[]{:S(2)}) async-start(bf16[8,2,16384]{2,1,0:T(2,128)(2,1)} %reshape.317), calls=%async_computation.4 | async-start | bytes 1048576 | tf_op jit(solution)/shard_map/all_to_all | solution.py:99
  296.5 0.3 reduce-scatter.2.cloned.1.call-start
  296.9 0.7 add_convert_fusion.1
  297.6 23.3 %reduce-scatter.2.cloned.1.call-done = bf16[2,8,1024]{2,1,0:T(8,128)(2,1)} async-done(((bf16[2,8,4096]{2,1,0:T(8,128)(2,1)}), bf16[2,8,1024]{2,1,0:T(8,128)(2,1)}) %reduce-scatter.2.cloned.1.call-update) | async-done | bytes 32784 | tf_op jit(solution)/shard_map/reduce_scatter | solution.py:103
  320.9 1.4 multiply_convert_fusion.6
  322.2 0.5 reshape.318
  322.8 3.3 reduce
  326.1 0.3 all_to_all.57
  326.4 0.3 copy.59
  326.7 1.2 reshape.232
  (31 shorter events, 0.5 us)
Async XLA Ops:
  7.2 33.8 %copy-start = (f32[16,32]{1,0:T(8,128)S(1)}, f32[16,32]{1,0:T(8,128)}, u32[]{:S(2)}) copy-start(f32[16,32]{1,0:T(8,128)} %param.12) | copy-start | bytes 6148
  10.0 21.8 %all-to-all-start = ((bf16[2,8,16384]{2,0,1:T(2,128)(2,1)}), bf16[2,8,16384]{2,0,1:T(2,128)(2,1)S(1)}, u32[]{:S(2)}, u32[]{:S(2)}) async-start(bf16[2,8,16384]{2,0,1:T(2,128)(2,1)} %copy.50), calls=%async_computation | async-start | bytes 1048576 | tf_op jit(solution)/shard_map/all_to_all | solution.py:49
  33.7 6.2 %copy-start.3 = (s32[2,16]{1,0:T(2,128)S(1)}, s32[2,16]{1,0:T(2,128)}, u32[]{:S(2)}) copy-start(s32[2,16]{1,0:T(2,128)} %param.13) | copy-start | bytes 388
  33.7 7.9 %copy-start.5 = (f32[2,8]{1,0:T(2,128)S(1)}, f32[2,8]{1,0:T(2,128)}, u32[]{:S(2)}) copy-start(f32[2,8]{1,0:T(2,128)} %param.11) | copy-start | bytes 196
  36.1 29.6 %all-to-all-start.1 = ((bf16[2,16,1,16384]{3,0,2,1:T(2,128)(2,1)}), bf16[2,16,1,16384]{3,0,2,1:T(2,128)(2,1)S(1)}, u32[]{:S(2)}, u32[]{:S(2)}) async-start(bf16[2,16,1,16384]{3,0,2,1:T(2,128)(2,1)} %copy.51), calls=%async_computation.1 | async-start | bytes 2097152 | tf_op jit(solution)/shard_map/all_to_all | solution.py:46
  39.7 90.2 %all-reduce.7.cloned.1.call-start = ((), (), s32[]{:S(2)}) async-start(), calls=%async_computation.7 | async-start | bytes 4194304 | tf_op jit(solution)/shard_map/psum | solution.py:72
  65.6 3.5 %copy-start.2 = (bf16[2,8,4096]{2,1,0:T(8,128)(2,1)S(1)}, bf16[2,8,4096]{2,1,0:T(8,128)(2,1)}, u32[]{:S(2)}) copy-start(bf16[2,8,4096]{2,1,0:T(8,128)(2,1)} %param.9) | copy-start | bytes 393220
  69.2 2.2 copy-start.1
  76.1 53.8 %copy-start.4 = (f32[2,512]{1,0:T(2,128)S(1)}, f32[2,512]{1,0:T(2,128)}, u32[]{:S(2)}) copy-start(f32[2,512]{1,0:T(2,128)} %param.14) | copy-start | bytes 12292
  79.3 156.7 %all-reduce.5.cloned.1.call-start = ((), (), s32[]{:S(2)}) async-start(), calls=%async_computation.6 | async-start | bytes 4194304 | tf_op jit(solution)/shard_map/psum | solution.py:72
  293.0 29.3 %all-to-all-start.3 = ((bf16[8,2,16384]{2,1,0:T(2,128)(2,1)}), bf16[8,2,16384]{2,1,0:T(2,128)(2,1)S(1)}, u32[]{:S(2)}, u32[]{:S(2)}) async-start(bf16[8,2,16384]{2,1,0:T(2,128)(2,1)} %reshape.317), calls=%async_computation.4 | async-start | bytes 1048576 | tf_op jit(solution)/shard_map/all_to_all | solution.py:99
  296.5 24.3 %reduce-scatter.2.cloned.1.call-start = ((), (), s32[]{:S(2)}) async-start(), calls=%async_computation.5 | async-start | bytes 163840 | tf_op jit(solution)/shard_map/reduce_scatter | solution.py:103
Sparse Core Ops, SparseCore 0:
  79.4 50.4 all-reduce.6
  133.5 102.3 all-reduce.4
  299.8 21.0 reduce-scatter.1
